TPU v7x, 32 devices: a whole 2x2x4 slice. The times are simulated.
32 devices in a mesh: blk: 8 (over z, x), tile: 4 (over y, core).
Axes of the slice: x: 2, y: 2, z: 4, core: 2. Of those that a mesh axis runs over, the one named last changes fastest.
Arguments:
- stream_in: bfloat16 [32, 16, 16, 2240], P('tile', 'blk'), may hold values from -6 to 6
- queries: bfloat16 [32, 16, 16, 2240], P('tile', 'blk'), may hold values from -12 to 12
- key_rows: bfloat16 [32, 16, 16, 2240], P('tile', 'blk'), may hold values from -12 to 12
- value_rows: bfloat16 [32, 16, 16, 2240], P('tile', 'blk'), may hold values from -12 to 12
- w_output: bfloat16 [2240, 2240], P('tile'), may hold values from -0.125 to 0.125
- w_inner: bfloat16 [2240, 2, 4096], P(None, None, 'tile'), may hold values from -0.125 to 0.125
- w_down: bfloat16 [4096, 2240], P('tile'), may hold values from -0.09375 to 0.09375
- spatial_taps: float32 [3, 3, 2, 4096], P(None, None, None, 'tile'), may hold values from -2 to 2
- temporal_taps: float32 [3, 2, 4096], P(None, None, 'tile'), may hold values from -3.5 to 3.5
Outputs:
- layer_out: bfloat16 [32, 16, 16, 2240], P('tile', 'blk')
All inputs are finite; a program needn't handle non-finite values.
Results may differ from a plain program's by a relative error of at most 0.009.
Values may be sent and summed in bfloat16 or wider, within the bound.
A program may use at most 128 MiB of HBM per device.

v0:
```python
import jax
import jax.numpy as jnp
from jax import lax
from jax.sharding import PartitionSpec as P

HEADS = 20
HEAD_DIM = 112
TAPS = 3
EPS = 1e-06


def from_partner(value, axis, stride):
    mask = 2**stride
    pairs = [(source, source ^ mask) for source in range(lax.axis_size(axis))]
    return lax.ppermute(value, axis, pairs)


def carried_in(x, axis, combine, identity):
    peers, position = (lax.axis_size(axis), lax.axis_index(axis))
    everything = jax.tree.map(lambda part: lax.all_gather(part, axis), x)
    start = jax.tree.map(
        lambda part, zero: jnp.broadcast_to(jnp.asarray(zero, part.dtype), part.shape), x, identity
    )

    def step(k, before):
        reached = k < position
        new = combine(before, jax.tree.map(lambda part: part[k], everything))
        return jax.tree.map(lambda a, b: jnp.where(reached, a, b), new, before)

    return lax.fori_loop(0, peers, step, start)


def shifted(x, axis, by):
    peers = lax.axis_size(axis)
    pairs = [(i, i + by) for i in range(peers) if 0 <= i + by < peers]
    return lax.ppermute(x, axis, pairs)


def add_pair(earlier, later):
    return (earlier[0] + later[0], earlier[1] + later[1])


def prefix_state(state_parts):
    partner = from_partner((state_parts[0], state_parts[1]), "blk", 0)
    block_sum = add_pair(state_parts, partner)
    odd_side = (lax.axis_index("blk") % 2).astype(jnp.float32)
    keep_share = 1.0 - 0.5 * odd_side
    zero_state = (jnp.zeros_like(block_sum[0]), jnp.zeros_like(block_sum[1]))
    before = carried_in((block_sum[0] * 0.5, block_sum[1] * 0.5), "blk", add_pair, zero_state)
    return (before[0] + block_sum[0] * keep_share, before[1] + block_sum[1] * keep_share)


def spatial_conv(inner_act, spatial_taps):
    row_count = inner_act.shape[0]
    col_count = inner_act.shape[2]
    padded = jnp.pad(inner_act, ((1, 1), (0, 0), (1, 1), (0, 0), (0, 0)))
    running = jnp.zeros(inner_act.shape, jnp.float32)
    for tap_row in range(3):
        for tap_col in range(3):
            window = padded[tap_row : tap_row + row_count, :, tap_col : tap_col + col_count]
            running = running + window.astype(jnp.float32) * spatial_taps[tap_row, tap_col]
    return running


def on_device(
    stream_in, queries, key_rows, value_rows, w_output, w_inner, w_down, spatial_taps, temporal_taps
):
    row_count, frames, col_count, model_width = queries.shape
    tokens = row_count * frames * col_count
    highest = lax.Precision.HIGHEST
    key_pos = jax.nn.relu(key_rows).reshape(tokens, HEADS, HEAD_DIM)
    value_heads = value_rows.reshape(tokens, HEADS, HEAD_DIM)
    local_kv = jnp.einsum("thd,the->hde", key_pos, value_heads, preferred_element_type=jnp.float32)
    local_kv = local_kv.reshape(model_width, HEAD_DIM)
    local_z = jnp.sum(key_pos.astype(jnp.float32), axis=0).reshape(model_width)
    shares = (
        lax.psum_scatter(local_kv, "tile", scatter_dimension=0, tiled=True),
        lax.psum_scatter(local_z, "tile", scatter_dimension=0, tiled=True),
    )
    share_state = prefix_state(shares)
    state, zsum = (
        lax.all_gather(share_state[0], "tile", axis=0, tiled=True),
        lax.all_gather(share_state[1], "tile", axis=0, tiled=True),
    )
    state = state.reshape(HEADS, HEAD_DIM, HEAD_DIM)
    zsum = zsum.reshape(HEADS, HEAD_DIM)
    query_pos = jax.nn.relu(queries.astype(jnp.float32)).reshape(tokens, HEADS, HEAD_DIM)
    numerator = jnp.einsum("thd,hde->the", query_pos, state, precision=highest)
    denominator = jnp.einsum("thd,hd->th", query_pos, zsum, precision=highest) + EPS
    attended = (numerator / denominator[..., None]).astype(jnp.bfloat16)
    attended = attended.reshape(row_count, frames, col_count, model_width)
    by_feature = lax.all_to_all(attended, "tile", split_axis=3, concat_axis=0, tiled=True)
    portion = by_feature
    product = jnp.dot(
        portion.reshape(-1, portion.shape[3]), w_output, preferred_element_type=jnp.float32
    )
    attn_out = lax.psum_scatter(
        product.reshape(row_count * lax.axis_size("tile"), frames, col_count, model_width),
        "tile",
        scatter_dimension=0,
        tiled=True,
    )
    hidden = (stream_in.astype(jnp.float32) + attn_out).astype(jnp.bfloat16)
    chan_dev = w_inner.shape[2]
    w_flat = w_inner.reshape(model_width, 2 * chan_dev)
    portion = lax.all_gather(hidden, "tile", axis=0, tiled=True)
    product = jnp.dot(portion.reshape(-1, model_width), w_flat, preferred_element_type=jnp.float32)
    activated = jax.nn.silu(product).astype(jnp.bfloat16)
    inner_act = activated.reshape(portion.shape[0], frames, col_count, 2, chan_dev)
    spatial = spatial_conv(inner_act, spatial_taps).astype(jnp.bfloat16)
    earlier_frames = shifted(spatial, "blk", 1)
    extended = jnp.concatenate([earlier_frames, spatial], axis=1)
    temporal_mix = jnp.zeros(spatial.shape, jnp.float32)
    for lag in range(TAPS):
        window = extended[:, TAPS - 1 - lag : TAPS - 1 - lag + frames]
        temporal_mix = temporal_mix + window.astype(jnp.float32) * temporal_taps[lag]
    gated_out = (temporal_mix[..., 0, :] * jax.nn.silu(temporal_mix[..., 1, :])).astype(
        jnp.bfloat16
    )
    portion = gated_out
    product = jnp.dot(portion.reshape(-1, chan_dev), w_down, preferred_element_type=jnp.float32)
    ffn_out = lax.psum_scatter(
        product.reshape(lax.axis_size("tile") * row_count, frames, col_count, model_width).astype(
            jnp.bfloat16
        ),
        "tile",
        scatter_dimension=0,
        tiled=True,
    ).astype(jnp.float32)
    return (hidden.astype(jnp.float32) + ffn_out).astype(jnp.bfloat16)


def solution(mesh):
    in_specs = (
        P("tile", "blk", None, None),
        P("tile", "blk", None, None),
        P("tile", "blk", None, None),
        P("tile", "blk", None, None),
        P("tile", None),
        P(None, None, "tile"),
        P("tile", None),
        P(None, None, None, "tile"),
        P(None, None, "tile"),
    )
    out_specs = P("tile", "blk", None, None)
    return jax.shard_map(
        on_device, mesh=mesh, in_specs=in_specs, out_specs=out_specs, check_vma=False
    )
```

profile of v0, /device:TPU:0, one launch (start us, length us, event | category | flops | bytes accessed | tf_op | source)
XLA Modules:
  0.0 571.9 jit_solution(4636084456415027600)
XLA Ops:
  6.5 2.5 broadcast_maximum_fusion
  9.1 4.0 reshape.58
  13.1 4.0 reshape.59
  17.1 3.5 fusion.8
  20.6 0.0 all-gather.7.cloned.1.call-start
  20.6 28.2 %reduce-scatter.4.cloned.1.call-done = f32[560,112]{1,0:T(8,128)} async-done(((f32[2240,112]{1,0:T(8,128)}), f32[560,112]{1,0:T(8,128)}) %reduce-scatter.4.cloned.1.call-update) | async-done | bytes 250896 | tf_op jit(solution)/shard_map/reduce_scatter | solution.py:77
  48.9 1.5 collective-permute-start
  50.3 7.2 %collective-permute-done = f32[560,112]{1,0:T(8,128)S(1)} collective-permute-done((f32[560,112]{1,0:T(8,128)}, f32[560,112]{1,0:T(8,128)S(1)}, u32[]{:S(2)}, u32[]{:S(2)}) %collective-permute-start) | collective-permute-done | bytes 250912 | tf_op jit(solution)/shard_map/ppermute | solution.py:15
  57.5 1.7 broadcast_multiply_fusion
  59.2 0.0 all-gather.7.cloned.1.call-update
  59.3 0.0 reduce-scatter.6.cloned.1.call-start
  59.3 0.7 fusion.13
  60.6 1.5 convert_reduce_fusion
  62.2 10.2 %all-reduce.3 = f32[2240]{0:T(1024)S(1)} all-reduce(f32[2240]{0:T(1024)S(1)} %convert_reduce_fusion), channel_id=5, replica_groups=mesh['blk'=8,'tile'=4] {'tile'}, use_global_device_ids=true, to_apply=%region_2.3.clone | all-reduce | flops 2240 | bytes 17920
  72.3 0.1 dynamic-slice.3
  72.4 1.9 collective-permute-start.1
  74.3 3.0 convert_maximum_fusion
  77.3 0.6 dynamic-slice
  79.2 4.3 reshape.62
  83.5 3.3 copy.27
  86.8 0.2 multiply_dynamic-update-slice_fusion
  87.0 36.8 %all-reduce.1 = f32[4480]{0:T(1024)S(1)} all-reduce(f32[4480]{0:T(1024)S(1)} %multiply_dynamic-update-slice_fusion), channel_id=3, replica_groups=mesh['blk'=8,'tile'=4] {'blk'}, use_global_device_ids=true, to_apply=%add.1 | all-reduce | flops 4480 | bytes 35840
  123.8 0.1 reshape.69
  123.9 0.0 all-gather.7.cloned.1.call-done
  123.9 8.9 %while.16 = (s32[]{:T(128)}, f32[560,112]{1,0:T(8,128)S(1)}, f32[560]{0:T(1024)S(1)}, s32[]{:T(128)}, f32[8,560,112]{2,1,0:T(8,128)}, /*index=5*/f32[8,560]{1,0:T(8,128)S(1)}, s32[]{:T(128)}, s32[]{:T(128)}) while((s32[]{:T(128)}, f32[560,112]{1,0:T(8,128)S(1)}, f32[560]{0:T(1024)S(1)}, s32[]{:T(128)}, f32[8,560,112]{2,1,0:T(8,128)}, ...), condition=%wide.region_4.5_spmd.clone, body=%wide.region_3.4_spmd.clone.sunk | while | flops 189844 | bytes 763955 | solution.py:30
  123.9 1.0 add_select_fusion.4
  125.0 1.0 add_select_fusion.4
  126.1 1.0 add_select_fusion.4
  127.3 1.0 add_select_fusion.4
  128.4 1.0 add_select_fusion.4
  129.5 1.0 add_select_fusion.4
  130.6 1.0 add_select_fusion.4
  131.7 1.0 add_select_fusion.4
  132.8 0.2 add_dynamic-update-slice_fusion
  133.0 10.1 %all-reduce.2 = f32[2240]{0:T(1024)S(1)} all-reduce(f32[2240]{0:T(1024)S(1)} %add_dynamic-update-slice_fusion), channel_id=1, replica_groups=mesh['blk'=8,'tile'=4] {'tile'}, use_global_device_ids=true, to_apply=%add.2 | all-reduce | flops 2240 | bytes 17920
  143.1 0.1 reshape.85
  143.2 3.0 fusion.14
  146.2 0.1 multiply_add_fusion.1
  146.3 9.7 %all_gather.25 = f32[2240,112]{1,0:T(8,128)S(1)} all-gather(f32[560,112]{1,0:T(8,128)S(1)} %multiply_add_fusion.1), channel_id=1, replica_groups=mesh['blk'=8,'tile'=4] {'tile'}, dimensions={0}, use_global_device_ids=true | all-gather | bytes 1254400 | tf_op jit(solution)/shard_map/all_gather | solution.py:82
  156.0 3.2 fusion.5
  159.2 28.0 %reshape.86 = bf16[8,2,16,2240]{2,1,0,3:T(2,128)(2,1)} reshape(bf16[256,20,112]{0,2,1:T(8,128)(2,1)} %fusion.5) | data formatting | bytes 2293760 | tf_op jit(solution)/shard_map/reshape | solution.py:91
  187.2 11.8 %reshape.89 = bf16[4,2,71680]{2,1,0:T(2,128)(2,1)} reshape(bf16[2240,8,2,16]{3,2,1,0:T(2,128)(2,1)} %bitcast.90) | data formatting | bytes 2293760
  198.9 19.8 %all_to_all.15 = bf16[4,2,71680]{2,1,0:T(2,128)(2,1)} all-to-all(bf16[4,2,71680]{2,1,0:T(2,128)(2,1)} %reshape.89), channel_id=1, replica_groups=mesh['blk'=8,'tile'=4] {'tile'}, dimensions={0} | all-to-all | bytes 2293760 | tf_op jit(solution)/shard_map/all_to_all | solution.py:92
  218.8 8.7 %reshape.90 = bf16[2240,8,2,16]{3,2,1,0:T(2,128)(2,1)} reshape(bf16[4,2,71680]{2,1,0:T(2,128)(2,1)} %all_to_all.15) | data formatting | bytes 2293760
  227.5 19.9 %copy.30 = bf16[8,2,16,4,560]{4,2,1,0,3:T(8,128)(2,1)} copy(bf16[8,2,16,4,560]{2,1,0,4,3:T(2,128)(2,1)} %bitcast.91) | data formatting | bytes 2293760 | tf_op jit(solution)/shard_map/all_to_all | solution.py:92
  247.3 7.8 %fusion.3 = f32[32,2,16,2240]{3,2,1,0:T(8,128)} fusion(bf16[32,2,16,560]{3,2,1,0:T(8,128)(2,1)} %bitcast.95, bf16[560,2240]{1,0:T(8,128)(2,1)S(1)} %copy-done), kind=kOutput, calls=%fused_computation.21 | convolution fusion | flops 2569011200 | bytes 12830720 | tf_op jit(solution)/shard_map/dot_general | solution.py:94
  255.2 0.0 reduce-scatter.6.cloned.1.call-update
  255.2 0.0 all-gather.5.cloned.1.call-start
  255.2 74.2 %reduce-scatter.6.cloned.1.call-done = f32[8,2,16,2240]{3,2,1,0:T(8,128)} async-done(((f32[32,2,16,2240]{3,2,1,0:T(8,128)}), f32[8,2,16,2240]{3,2,1,0:T(8,128)}) %reduce-scatter.6.cloned.1.call-update) | async-done | bytes 2293776 | tf_op jit(solution)/shard_map/reduce_scatter | solution.py:97
  329.4 2.9 add_convert_fusion.2
  332.3 0.0 all-gather.5.cloned.1.call-update
  332.4 0.3 reduce-scatter.8.cloned.1.call-start
  332.6 11.4 %copy.38 = bf16[280,8,2,1024]{3,1,2,0:T(8,128)(2,1)} copy(bf16[280,8,2,1024]{3,2,1,0:T(2,128)(2,1)} %bitcast.92) | data formatting | bytes 18350080
  344.1 25.9 %all-gather.5.cloned.1.call-done = bf16[32,2,16,2240]{3,2,1,0:T(8,128)(2,1)} async-done(((bf16[8,2,16,2240]{3,2,1,0:T(8,128)(2,1)}), bf16[32,2,16,2240]{3,2,1,0:T(8,128)(2,1)}) %all-gather.5.cloned.1.call-update) | async-done | bytes 4587536 | tf_op jit(solution)/shard_map/all_gather | solution.py:106
  370.0 16.0 %multiply_convert_fusion = bf16[1024,2048]{1,0:T(8,128)(2,1)} fusion(bf16[1024,2240]{1,0:T(8,128)(2,1)} %bitcast.98, bf16[2240,2048]{1,0:T(8,128)(2,1)} %bitcast.93), kind=kOutput, calls=%fused_computation.13 | convolution fusion | flops 9405726720 | bytes 17956864 | tf_op jit(solution)/shard_map/dot_general | solution.py:107
  386.0 7.8 %reshape.67 = bf16[32,2,16,2,1024]{4,3,2,1,0:T(2,128)(2,1)} reshape(bf16[1024,2048]{1,0:T(8,128)(2,1)} %multiply_convert_fusion) | data formatting | bytes 8388608 | tf_op jit(solution)/shard_map/reshape | solution.py:109
  393.8 3.5 copy.31
  397.3 11.9 %add_convert_fusion = bf16[32,2,16,2,1024]{4,2,1,0,3:T(8,128)(2,1)S(1)} fusion(bf16[32,2,16,2,1024]{4,2,1,0,3:T(8,128)(2,1)S(1)} %copy.31, f32[2,1024]{1,0:T(2,128)S(1)} %get-tuple-element.157, f32[2,1024]{1,0:T(2,128)S(1)} %get-tuple-element.158, f32[2,1024]{1,0:T(2,128)S(1)} %get-tuple-element.151, f32[2,1024]{1,0:T(2,128)S(1)} %get-tuple-element.152, ...), kind=kLoop, calls=%fused_computation.12 | loop fusion | flops 56623104 | bytes 8462336 | tf_op jit(solution)/shard_map/convert_element_type | solution.py:110
  409.2 3.9 collective-permute-start.2
  413.2 89.7 %collective-permute-done.2 = bf16[32,2,16,2,1024]{4,2,1,0,3:T(8,128)(2,1)S(1)} collective-permute-done((bf16[32,2,16,2,1024]{4,2,1,0,3:T(8,128)(2,1)S(1)}, bf16[32,2,16,2,1024]{4,2,1,0,3:T(8,128)(2,1)S(1)}, u32[]{:S(2)}, u32[]{:S(2)}) %collective-permute-start.2) | collective-permute-done | bytes 4194336 | tf_op jit(solution)/shard_map/ppermute | solution.py:36
  502.8 3.2 multiply_add_fusion
  506.0 7.3 %convolution_convert_fusion = bf16[32,2,16,2240]{3,2,1,0:T(8,128)(2,1)} fusion(bf16[1024,2240]{0,1:T(8,128)(2,1)S(1)} %bitcast.100, f32[32,2,16,2,1024]{4,2,1,0,3:T(8,128)S(1)} %multiply_add_fusion), kind=kOutput, calls=%fused_computation.14 | convolution fusion | flops 4706205696 | bytes 17563648 | tf_op jit(solution)/shard_map/dot_general | solution.py:121
  513.4 49.1 %reduce-scatter.8.cloned.1.call-done = bf16[8,2,16,2240]{3,2,1,0:T(8,128)(2,1)} async-done(((bf16[32,2,16,2240]{3,2,1,0:T(8,128)(2,1)}), bf16[8,2,16,2240]{3,2,1,0:T(8,128)(2,1)}) %reduce-scatter.8.cloned.1.call-update) | async-done | bytes 1146896 | tf_op jit(solution)/shard_map/reduce_scatter | solution.py:122
  562.5 2.9 add_convert_fusion.1
  (50 shorter events, 0.3 us)
Async XLA Ops:
  6.5 240.8 %copy-start = (bf16[560,2240]{1,0:T(8,128)(2,1)S(1)}, bf16[560,2240]{1,0:T(8,128)(2,1)}, u32[]{:S(2)}) copy-start(bf16[560,2240]{1,0:T(8,128)(2,1)} %param.15) | copy-start | bytes 7526404
  6.5 42.3 %reduce-scatter.4.cloned.1.call-start = ((), (), s32[]{:S(2)}) async-start(), calls=%async_computation.4 | async-start | bytes 1433600 | tf_op jit(solution)/shard_map/reduce_scatter | solution.py:77
  13.1 46.2 %copy-start.7 = (u32[32]{0:T(128)S(1)}, u32[32]{0:T(128)}, u32[]{:S(2)}) copy-start(u32[32]{0:T(128)} %constant.77) | copy-start | bytes 388
  20.6 56.7 %copy-start.8 = (u32[32]{0:T(128)S(1)}, u32[32]{0:T(128)}, u32[]{:S(2)}) copy-start(u32[32]{0:T(128)} %constant.72) | copy-start | bytes 388
  20.6 103.3 %all-gather.7.cloned.1.call-start = ((), (), s32[]{:S(2)}) async-start(), calls=%async_computation.8 | async-start | bytes 2580480 | tf_op jit(solution)/shard_map/all_gather | solution.py:20
  48.9 8.6 %collective-permute-start = (f32[560,112]{1,0:T(8,128)}, f32[560,112]{1,0:T(8,128)S(1)}, u32[]{:S(2)}, u32[]{:S(2)}) collective-permute-start(f32[560,112]{1,0:T(8,128)} %reduce-scatter.4.cloned.1.call-done), channel_id=1, source_target_pairs={{0,4},{4,0},{8,12},{12,8},{16,20},{20,16},{24,28},{28,24},{1,5},{5... | collective-permute-start | bytes 752648 | tf_op jit(solution)/shard_map/ppermute | solution.py:15
  59.3 270.2 %reduce-scatter.6.cloned.1.call-start = ((), (), s32[]{:S(2)}) async-start(), calls=%async_computation.5 | async-start | bytes 11796480 | tf_op jit(solution)/shard_map/reduce_scatter | solution.py:97
  72.4 14.4 %collective-permute-start.1 = (f32[560]{0:T(1024)S(1)}, f32[560]{0:T(1024)S(1)}, u32[]{:S(2)}, u32[]{:S(2)}) collective-permute-start(f32[560]{0:T(1024)S(1)} %dynamic-slice.3), channel_id=1, source_target_pairs={{0,4},{4,0},{8,12},{12,8},{16,20},{20,16},{24,28},{28,24},{1,5},{5... | collective-permute-start | bytes 6728 | tf_op jit(solution)/shard_map/ppermute | solution.py:15
  86.8 59.4 %copy-start.4 = (f32[560,112]{1,0:T(8,128)S(1)}, f32[560,112]{1,0:T(8,128)}, u32[]{:S(2)}) copy-start(f32[560,112]{1,0:T(8,128)} %reduce-scatter.4.cloned.1.call-done) | copy-start | bytes 752644
  143.2 12.8 %copy-start.2 = (f32[256,20,112]{0,2,1:T(8,128)S(1)}, f32[256,20,112]{0,2,1:T(8,128)}, u32[]{:S(2)}) copy-start(f32[256,20,112]{0,2,1:T(8,128)} %copy.27) | copy-start | bytes 6881284
  255.2 74.3 %copy-start.3 = (bf16[8,2,16,2240]{3,2,1,0:T(8,128)(2,1)S(1)}, bf16[8,2,16,2240]{3,2,1,0:T(8,128)(2,1)}, u32[]{:S(2)}) copy-start(bf16[8,2,16,2240]{3,2,1,0:T(8,128)(2,1)} %param.11) | copy-start | bytes 3440644
  255.2 114.8 %all-gather.5.cloned.1.call-start = ((), (), s32[]{:S(2)}) async-start(), calls=%async_computation.6 | async-start | bytes 5898240 | tf_op jit(solution)/shard_map/all_gather | solution.py:106
  332.4 230.1 %reduce-scatter.8.cloned.1.call-start = ((), (), s32[]{:S(2)}) async-start(), calls=%async_computation.7 | async-start | bytes 5898240 | tf_op jit(solution)/shard_map/reduce_scatter | solution.py:122
  332.6 11.4 %copy-start.5 = (f32[3,3,2,1024]{3,2,1,0:T(2,128)S(1)}, f32[3,3,2,1024]{3,2,1,0:T(2,128)}, u32[]{:S(2)}) copy-start(f32[3,3,2,1024]{3,2,1,0:T(2,128)} %param.18) | copy-start | bytes 221188
  397.3 15.8 %copy-start.6 = (f32[3,2,1024]{2,1,0:T(2,128)S(1)}, f32[3,2,1024]{2,1,0:T(2,128)}, u32[]{:S(2)}) copy-start(f32[3,2,1024]{2,1,0:T(2,128)} %param.19) | copy-start | bytes 73732
  397.3 108.7 %slice-start = ((s8[4587520]{0:T(1024)(128)(4,1)}), s8[4194304]{0:T(1024)(128)(4,1)S(1)}, s32[]{:S(2)}) async-start(s8[4587520]{0:T(1024)(128)(4,1)} %bitcast.99), calls=%async_computation.9 | async-start | bytes 8388608
  409.2 93.6 %collective-permute-start.2 = (bf16[32,2,16,2,1024]{4,2,1,0,3:T(8,128)(2,1)S(1)}, bf16[32,2,16,2,1024]{4,2,1,0,3:T(8,128)(2,1)S(1)}, u32[]{:S(2)}, u32[]{:S(2)}) collective-permute-start(bf16[32,2,16,2,1024]{4,2,1,0,3:T(8,128)(2,1)S(1)} %add_convert_fusion), channel_id=1, source_target_pairs={{0,4},{4,8},{8,12},{12,16},{16,20},{20,24},{24,28},{1,5},{5,9},{9,... | collective-permute-start | bytes 12582920 | tf_op jit(solution)/shard_map/ppermute | solution.py:36
  502.8 3.2 slice-start.1
  506.0 59.4 %copy-start.1 = (bf16[560,2240]{1,0:T(8,128)(2,1)S(1)}, bf16[560,2240]{1,0:T(8,128)(2,1)}, u32[]{:S(2)}) copy-start(bf16[560,2240]{1,0:T(8,128)(2,1)} %param.15) | copy-start | bytes 7526404
Sparse Core Ops, SparseCore 0:
  20.7 28.1 reduce-scatter.3
  59.4 51.7 all-gather.6
  255.3 74.0 reduce-scatter.5
  332.5 37.4 all-gather.4
  513.5 48.9 reduce-scatter.7
where the time goes:
time: 574 us; the launch traced here: 572 us
  waiting for transfers between devices  274 us (48%)
  local copies, waits for them, and re-layouts  108 us (19%)
  blocking collectives  86.6 us (15%)
  matrix products  40.7 us (7%)
  other arithmetic  38.5 us (7%)
  between operations  15.2 us (3%)
  starting transfers between devices  7.66 us (1%)
    ppermute x1, waiting for transfers between devices, shifted(): return lax.ppermute(x, axis, pairs)  89.7 us
    reduce_scatter x1, waiting for transfers between devices, on_device(): lax.psum_scatter(product.reshape(row_count * lax.axis_size('tile'), frame...  74.2 us
    unnamed x3, blocking collectives  57.1 us
    reduce_scatter x1, waiting for transfers between devices, on_device(): lax.psum_scatter(product.reshape(lax.axis_size('tile') * row_count, frame...  49.1 us
    unnamed x30, local copies, waits for them, and re-layouts  33.3 us
    reduce_scatter x1, waiting for transfers between devices, on_device(): lax.psum_scatter(local_kv, 'tile', scatter_dimension=0, tiled=True)  28.2 us
    reshape x1, local copies, waits for them, and re-layouts, on_device(): attended = attended.reshape(row_count, frames, col_count, model_width)  28 us
    all_gather x1, waiting for transfers between devices, on_device(): portion = lax.all_gather(hidden, 'tile', axis=0, tiled=True)  25.9 us
  transfers between devices with their start and end apart: 8, of which 6 were waited for; matrix products, arithmetic and copies ran while one was open for 4% of the time, Pallas kernels for 0%

commit v1 on v0

--- a/solution.py
+++ b/solution.py
@@ -89,7 +89,10 @@
     denominator = jnp.einsum("thd,hd->th", query_pos, zsum, precision=highest) + EPS
     attended = (numerator / denominator[..., None]).astype(jnp.bfloat16)
     attended = attended.reshape(row_count, frames, col_count, model_width)
-    by_feature = lax.all_to_all(attended, "tile", split_axis=3, concat_axis=0, tiled=True)
+    by_feature = jnp.concatenate(
+        lax.all_to_all(jnp.stack(jnp.split(attended, lax.axis_size("tile"), axis=3)), "tile", 0, 0),
+        axis=0,
+    )
     portion = by_feature
     product = jnp.dot(
         portion.reshape(-1, portion.shape[3]), w_output, preferred_element_type=jnp.float32

time: 574 us -> 512 us (0.89)
  local copies, waits for them, and re-layouts: 108 us -> 48.3 us
    reshape x1, local copies, waits for them, and re-layouts: 28 us -> 3.66 us  [on_device(): attended = attended.reshape(row_count, frames, col_count, model_width)]
    unnamed x30 -> x28, local copies, waits for them, and re-layouts: 33.3 us -> 12.8 us
    all_to_all x1 -> x0, local copies, waits for them, and re-layouts: 19.9 us -> none  [on_device(): lax.all_to_all(attended, 'tile', split_axis=3, concat_axis=0, tiled=True)]
  transfers between devices with their start and end apart: 8 -> 8, of which waited for: 6 -> 6; matrix products, arithmetic and copies ran while one was open for 4% -> 5% of each run, Pallas kernels for 0% -> 0%
where the time goes in v1:
time: 512 us; the launch traced here: 511 us
  waiting for transfers between devices  274 us (54%)
  blocking collectives  86.7 us (17%)
  local copies, waits for them, and re-layouts  48.3 us (9%)
  matrix products  39.2 us (8%)
  other arithmetic  38.9 us (8%)
  between operations  15.2 us (3%)
  starting transfers between devices  7.66 us (1%)
    ppermute x1, waiting for transfers between devices, shifted(): return lax.ppermute(x, axis, pairs)  89.7 us
    reduce_scatter x1, waiting for transfers between devices, on_device(): lax.psum_scatter(product.reshape(row_count * lax.axis_size('tile'), frame...  74.2 us
    unnamed x3, blocking collectives  57.1 us
    reduce_scatter x1, waiting for transfers between devices, on_device(): lax.psum_scatter(product.reshape(lax.axis_size('tile') * row_count, frame...  49.1 us
    reduce_scatter x1, waiting for transfers between devices, on_device(): lax.psum_scatter(local_kv, 'tile', scatter_dimension=0, tiled=True)  28.2 us
    all_gather x1, waiting for transfers between devices, on_device(): portion = lax.all_gather(hidden, 'tile', axis=0, tiled=True)  25.9 us
    all_to_all x1, blocking collectives, on_device(): lax.all_to_all(jnp.stack(jnp.split(attended, lax.axis_size('tile'), axis=...  19.9 us
    dot_general x1, matrix products, on_device(): jnp.dot(portion.reshape(-1, model_width), w_flat, preferred_element_type=...  16 us
  transfers between devices with their start and end apart: 8, of which 6 were waited for; matrix products, arithmetic and copies ran while one was open for 5% of the time, Pallas kernels for 0%

profile of v1, /device:TPU:0, one launch (start us, length us, event | category | flops | bytes accessed | tf_op | source)
XLA Modules:
  0.0 510.6 jit_solution(3814639003826604296)
XLA Ops:
  6.5 2.5 broadcast_maximum_fusion
  9.1 4.0 reshape.56
  13.1 4.0 reshape.57
  17.1 3.5 fusion.8
  20.6 0.0 reduce-scatter.4.cloned.1.call-update
  20.6 0.0 all-gather.7.cloned.1.call-start
  20.7 28.2 %reduce-scatter.4.cloned.1.call-done = f32[560,112]{1,0:T(8,128)} async-done(((f32[2240,112]{1,0:T(8,128)}), f32[560,112]{1,0:T(8,128)}) %reduce-scatter.4.cloned.1.call-update) | async-done | bytes 250896 | tf_op jit(solution)/shard_map/reduce_scatter | solution.py:77
  48.9 1.5 collective-permute-start
  50.4 7.2 %collective-permute-done = f32[560,112]{1,0:T(8,128)S(1)} collective-permute-done((f32[560,112]{1,0:T(8,128)}, f32[560,112]{1,0:T(8,128)S(1)}, u32[]{:S(2)}, u32[]{:S(2)}) %collective-permute-start) | collective-permute-done | bytes 250912 | tf_op jit(solution)/shard_map/ppermute | solution.py:15
  57.5 1.7 broadcast_multiply_fusion
  59.2 0.0 all-gather.7.cloned.1.call-update
  59.3 0.0 reduce-scatter.6.cloned.1.call-start
  59.3 0.6 fusion.13
  60.5 1.5 convert_reduce_fusion
  62.0 10.2 %all-reduce.3 = f32[2240]{0:T(1024)S(1)} all-reduce(f32[2240]{0:T(1024)S(1)} %convert_reduce_fusion), channel_id=5, replica_groups=mesh['blk'=8,'tile'=4] {'tile'}, use_global_device_ids=true, to_apply=%region_2.3.clone | all-reduce | flops 2240 | bytes 17920
  72.2 0.1 dynamic-slice.3
  72.3 1.9 collective-permute-start.1
  74.2 3.0 convert_maximum_fusion
  77.2 0.7 dynamic-slice
  79.2 4.3 reshape.60
  83.5 3.3 copy.26
  86.8 0.2 multiply_dynamic-update-slice_fusion
  87.0 36.8 %all-reduce.1 = f32[4480]{0:T(1024)S(1)} all-reduce(f32[4480]{0:T(1024)S(1)} %multiply_dynamic-update-slice_fusion), channel_id=3, replica_groups=mesh['blk'=8,'tile'=4] {'blk'}, use_global_device_ids=true, to_apply=%add.1 | all-reduce | flops 4480 | bytes 35840
  123.8 0.1 reshape.67
  123.9 0.0 all-gather.7.cloned.1.call-done
  123.9 8.9 %while.16 = (s32[]{:T(128)}, f32[560,112]{1,0:T(8,128)S(1)}, f32[560]{0:T(1024)S(1)}, s32[]{:T(128)}, f32[8,560,112]{2,1,0:T(8,128)}, /*index=5*/f32[8,560]{1,0:T(8,128)S(1)}, s32[]{:T(128)}, s32[]{:T(128)}) while((s32[]{:T(128)}, f32[560,112]{1,0:T(8,128)S(1)}, f32[560]{0:T(1024)S(1)}, s32[]{:T(128)}, f32[8,560,112]{2,1,0:T(8,128)}, ...), condition=%wide.region_4.5_spmd.clone, body=%wide.region_3.4_spmd.clone.sunk | while | flops 189844 | bytes 763955 | solution.py:30
  123.9 1.0 add_select_fusion.4
  125.0 1.0 add_select_fusion.4
  126.1 1.0 add_select_fusion.4
  127.2 1.0 add_select_fusion.4
  128.4 1.0 add_select_fusion.4
  129.5 1.0 add_select_fusion.4
  130.6 1.0 add_select_fusion.4
  131.7 1.0 add_select_fusion.4
  132.8 0.2 add_dynamic-update-slice_fusion
  133.0 10.1 %all-reduce.2 = f32[2240]{0:T(1024)S(1)} all-reduce(f32[2240]{0:T(1024)S(1)} %add_dynamic-update-slice_fusion), channel_id=1, replica_groups=mesh['blk'=8,'tile'=4] {'tile'}, use_global_device_ids=true, to_apply=%add.2 | all-reduce | flops 2240 | bytes 17920
  143.1 0.1 reshape.83
  143.2 3.0 fusion.14
  146.2 0.1 multiply_add_fusion.1
  146.3 9.6 %all_gather.25 = f32[2240,112]{1,0:T(8,128)S(1)} all-gather(f32[560,112]{1,0:T(8,128)S(1)} %multiply_add_fusion.1), channel_id=1, replica_groups=mesh['blk'=8,'tile'=4] {'tile'}, dimensions={0}, use_global_device_ids=true | all-gather | bytes 1254400 | tf_op jit(solution)/shard_map/all_gather | solution.py:82
  155.9 3.3 fusion.5
  159.2 2.7 copy.27
  161.9 3.7 reshape.62
  165.6 1.8 slice_bitcast_fusion.5
  167.4 0.3 pad_maximum_fusion.1
  167.6 19.9 %all_to_all.5 = bf16[4,8,2,16,560]{4,3,2,1,0:T(8,128)(2,1)S(1)} all-to-all(bf16[4,8,2,16,560]{4,3,2,1,0:T(8,128)(2,1)S(1)} %pad_maximum_fusion.1), channel_id=1, replica_groups=mesh['blk'=8,'tile'=4] {'tile'}, dimensions={0} | all-to-all | bytes 2293760 | tf_op jit(solution)/shard_map/all_to_all | solution.py:93
  187.6 6.2 %fusion.3 = f32[32,2,16,2240]{3,2,1,0:T(8,128)} fusion(bf16[32,2,16,560]{3,2,1,0:T(8,128)(2,1)S(1)} %bitcast.94, bf16[560,2240]{1,0:T(8,128)(2,1)S(1)} %copy-done), kind=kOutput, calls=%fused_computation.21 | convolution fusion | flops 2569011200 | bytes 12830720 | tf_op jit(solution)/shard_map/dot_general | solution.py:97
  193.8 0.0 reduce-scatter.6.cloned.1.call-update
  193.8 0.0 all-gather.5.cloned.1.call-start
  193.9 74.2 %reduce-scatter.6.cloned.1.call-done = f32[8,2,16,2240]{3,2,1,0:T(8,128)} async-done(((f32[32,2,16,2240]{3,2,1,0:T(8,128)}), f32[8,2,16,2240]{3,2,1,0:T(8,128)}) %reduce-scatter.6.cloned.1.call-update) | async-done | bytes 2293776 | tf_op jit(solution)/shard_map/reduce_scatter | solution.py:100
  268.0 2.9 add_convert_fusion.2
  271.0 0.3 reduce-scatter.8.cloned.1.call-start
  271.3 11.4 %copy.35 = bf16[280,8,2,1024]{3,1,2,0:T(8,128)(2,1)} copy(bf16[280,8,2,1024]{3,2,1,0:T(2,128)(2,1)} %bitcast.91) | data formatting | bytes 18350080
  282.7 25.9 %all-gather.5.cloned.1.call-done = bf16[32,2,16,2240]{3,2,1,0:T(8,128)(2,1)} async-done(((bf16[8,2,16,2240]{3,2,1,0:T(8,128)(2,1)}), bf16[32,2,16,2240]{3,2,1,0:T(8,128)(2,1)}) %all-gather.5.cloned.1.call-update) | async-done | bytes 4587536 | tf_op jit(solution)/shard_map/all_gather | solution.py:109
  308.6 16.0 %multiply_convert_fusion = bf16[1024,2048]{1,0:T(8,128)(2,1)} fusion(bf16[1024,2240]{1,0:T(8,128)(2,1)} %bitcast.97, bf16[2240,2048]{1,0:T(8,128)(2,1)} %bitcast.92), kind=kOutput, calls=%fused_computation.13 | convolution fusion | flops 9405726720 | bytes 17956864 | tf_op jit(solution)/shard_map/dot_general | solution.py:110
  324.6 7.8 %reshape.65 = bf16[32,2,16,2,1024]{4,3,2,1,0:T(2,128)(2,1)} reshape(bf16[1024,2048]{1,0:T(8,128)(2,1)} %multiply_convert_fusion) | data formatting | bytes 8388608 | tf_op jit(solution)/shard_map/reshape | solution.py:112
  332.4 3.5 copy.28
  335.9 12.0 %add_convert_fusion = bf16[32,2,16,2,1024]{4,2,1,0,3:T(8,128)(2,1)S(1)} fusion(bf16[32,2,16,2,1024]{4,2,1,0,3:T(8,128)(2,1)S(1)} %copy.28, f32[2,1024]{1,0:T(2,128)S(1)} %get-tuple-element.161, f32[2,1024]{1,0:T(2,128)S(1)} %get-tuple-element.162, f32[2,1024]{1,0:T(2,128)S(1)} %get-tuple-element.155, f32[2,1024]{1,0:T(2,128)S(1)} %get-tuple-element.156, ...), kind=kLoop, calls=%fused_computation.12 | loop fusion | flops 56623104 | bytes 8462336 | tf_op jit(solution)/shard_map/convert_element_type | solution.py:113
  347.9 3.9 collective-permute-start.2
  351.9 89.7 %collective-permute-done.2 = bf16[32,2,16,2,1024]{4,2,1,0,3:T(8,128)(2,1)S(1)} collective-permute-done((bf16[32,2,16,2,1024]{4,2,1,0,3:T(8,128)(2,1)S(1)}, bf16[32,2,16,2,1024]{4,2,1,0,3:T(8,128)(2,1)S(1)}, u32[]{:S(2)}, u32[]{:S(2)}) %collective-permute-start.2) | collective-permute-done | bytes 4194336 | tf_op jit(solution)/shard_map/ppermute | solution.py:36
  441.5 3.2 multiply_add_fusion
  444.7 7.2 %convolution_convert_fusion = bf16[32,2,16,2240]{3,2,1,0:T(8,128)(2,1)} fusion(bf16[1024,2240]{0,1:T(8,128)(2,1)S(1)} %bitcast.99, f32[32,2,16,2,1024]{4,2,1,0,3:T(8,128)S(1)} %multiply_add_fusion), kind=kOutput, calls=%fused_computation.14 | convolution fusion | flops 4706205696 | bytes 17563648 | tf_op jit(solution)/shard_map/dot_general | solution.py:124
  452.0 49.1 %reduce-scatter.8.cloned.1.call-done = bf16[8,2,16,2240]{3,2,1,0:T(8,128)(2,1)} async-done(((bf16[32,2,16,2240]{3,2,1,0:T(8,128)(2,1)}), bf16[8,2,16,2240]{3,2,1,0:T(8,128)(2,1)}) %reduce-scatter.8.cloned.1.call-update) | async-done | bytes 1146896 | tf_op jit(solution)/shard_map/reduce_scatter | solution.py:125
  501.1 2.9 add_convert_fusion.1
  (50 shorter events, 0.3 us)
Async XLA Ops:
  6.5 181.0 %copy-start = (bf16[560,2240]{1,0:T(8,128)(2,1)S(1)}, bf16[560,2240]{1,0:T(8,128)(2,1)}, u32[]{:S(2)}) copy-start(bf16[560,2240]{1,0:T(8,128)(2,1)} %param.15) | copy-start | bytes 7526404
  6.5 42.4 %reduce-scatter.4.cloned.1.call-start = ((), (), s32[]{:S(2)}) async-start(), calls=%async_computation.4 | async-start | bytes 1433600 | tf_op jit(solution)/shard_map/reduce_scatter | solution.py:77
  13.1 46.2 %copy-start.7 = (u32[32]{0:T(128)S(1)}, u32[32]{0:T(128)}, u32[]{:S(2)}) copy-start(u32[32]{0:T(128)} %constant.77) | copy-start | bytes 388
  20.6 56.6 %copy-start.8 = (u32[32]{0:T(128)S(1)}, u32[32]{0:T(128)}, u32[]{:S(2)}) copy-start(u32[32]{0:T(128)} %constant.72) | copy-start | bytes 388
  20.6 103.3 %all-gather.7.cloned.1.call-start = ((), (), s32[]{:S(2)}) async-start(), calls=%async_computation.8 | async-start | bytes 2580480 | tf_op jit(solution)/shard_map/all_gather | solution.py:20
  48.9 8.6 %collective-permute-start = (f32[560,112]{1,0:T(8,128)}, f32[560,112]{1,0:T(8,128)S(1)}, u32[]{:S(2)}, u32[]{:S(2)}) collective-permute-start(f32[560,112]{1,0:T(8,128)} %reduce-scatter.4.cloned.1.call-done), channel_id=1, source_target_pairs={{0,4},{4,0},{8,12},{12,8},{16,20},{20,16},{24,28},{28,24},{1,5},{5... | collective-permute-start | bytes 752648 | tf_op jit(solution)/shard_map/ppermute | solution.py:15
  59.3 208.8 %reduce-scatter.6.cloned.1.call-start = ((), (), s32[]{:S(2)}) async-start(), calls=%async_computation.5 | async-start | bytes 11796480 | tf_op jit(solution)/shard_map/reduce_scatter | solution.py:100
  72.3 14.5 %collective-permute-start.1 = (f32[560]{0:T(1024)S(1)}, f32[560]{0:T(1024)S(1)}, u32[]{:S(2)}, u32[]{:S(2)}) collective-permute-start(f32[560]{0:T(1024)S(1)} %dynamic-slice.3), channel_id=1, source_target_pairs={{0,4},{4,0},{8,12},{12,8},{16,20},{20,16},{24,28},{28,24},{1,5},{5... | collective-permute-start | bytes 6728 | tf_op jit(solution)/shard_map/ppermute | solution.py:15
  86.8 59.4 %copy-start.4 = (f32[560,112]{1,0:T(8,128)S(1)}, f32[560,112]{1,0:T(8,128)}, u32[]{:S(2)}) copy-start(f32[560,112]{1,0:T(8,128)} %reduce-scatter.4.cloned.1.call-done) | copy-start | bytes 752644
  143.2 12.7 %copy-start.2 = (f32[256,20,112]{0,2,1:T(8,128)S(1)}, f32[256,20,112]{0,2,1:T(8,128)}, u32[]{:S(2)}) copy-start(f32[256,20,112]{0,2,1:T(8,128)} %copy.26) | copy-start | bytes 6881284
  193.8 74.3 %copy-start.3 = (bf16[8,2,16,2240]{3,2,1,0:T(8,128)(2,1)S(1)}, bf16[8,2,16,2240]{3,2,1,0:T(8,128)(2,1)}, u32[]{:S(2)}) copy-start(bf16[8,2,16,2240]{3,2,1,0:T(8,128)(2,1)} %param.11) | copy-start | bytes 3440644
  193.8 114.8 %all-gather.5.cloned.1.call-start = ((), (), s32[]{:S(2)}) async-start(), calls=%async_computation.6 | async-start | bytes 5898240 | tf_op jit(solution)/shard_map/all_gather | solution.py:109
  271.0 230.2 %reduce-scatter.8.cloned.1.call-start = ((), (), s32[]{:S(2)}) async-start(), calls=%async_computation.7 | async-start | bytes 5898240 | tf_op jit(solution)/shard_map/reduce_scatter | solution.py:125
  271.2 11.4 %copy-start.5 = (f32[3,3,2,1024]{3,2,1,0:T(2,128)S(1)}, f32[3,3,2,1024]{3,2,1,0:T(2,128)}, u32[]{:S(2)}) copy-start(f32[3,3,2,1024]{3,2,1,0:T(2,128)} %param.18) | copy-start | bytes 221188
  335.9 15.9 %copy-start.6 = (f32[3,2,1024]{2,1,0:T(2,128)S(1)}, f32[3,2,1024]{2,1,0:T(2,128)}, u32[]{:S(2)}) copy-start(f32[3,2,1024]{2,1,0:T(2,128)} %param.19) | copy-start | bytes 73732
  335.9 108.8 %slice-start = ((s8[4587520]{0:T(1024)(128)(4,1)}), s8[4194304]{0:T(1024)(128)(4,1)S(1)}, s32[]{:S(2)}) async-start(s8[4587520]{0:T(1024)(128)(4,1)} %bitcast.98), calls=%async_computation.9 | async-start | bytes 8388608
  347.9 93.6 %collective-permute-start.2 = (bf16[32,2,16,2,1024]{4,2,1,0,3:T(8,128)(2,1)S(1)}, bf16[32,2,16,2,1024]{4,2,1,0,3:T(8,128)(2,1)S(1)}, u32[]{:S(2)}, u32[]{:S(2)}) collective-permute-start(bf16[32,2,16,2,1024]{4,2,1,0,3:T(8,128)(2,1)S(1)} %add_convert_fusion), channel_id=1, source_target_pairs={{0,4},{4,8},{8,12},{12,16},{16,20},{20,24},{24,28},{1,5},{5,9},{9,... | collective-permute-start | bytes 12582920 | tf_op jit(solution)/shard_map/ppermute | solution.py:36
  441.5 3.2 slice-start.1
  444.7 59.3 %copy-start.1 = (bf16[560,2240]{1,0:T(8,128)(2,1)S(1)}, bf16[560,2240]{1,0:T(8,128)(2,1)}, u32[]{:S(2)}) copy-start(bf16[560,2240]{1,0:T(8,128)(2,1)} %param.15) | copy-start | bytes 7526404
Sparse Core Ops, SparseCore 0:
  20.7 28.1 reduce-scatter.3
  59.4 51.7 all-gather.6
  193.9 74.0 reduce-scatter.5
  271.1 37.4 all-gather.4
  452.1 48.9 reduce-scatter.7
